TPU v7x, 512 devices: a whole 4x8x8 slice. The times are simulated.
512 devices in a mesh: mem: 8 (over z_lo, core), space: 64 (over z_hi, x, y).
Axes of the slice: x: 4, y: 8, z: 8 (z_hi: 2, z_lo: 4; z = z_hi * 4 + z_lo), core: 2. Of those that a mesh axis runs over, the one named last changes fastest.
Arguments:
- log_perm: float32 [128, 128, 2048], P('space', 'mem'), may hold values from -2 to 2
- concentration: float32 [128, 128, 2048], P('space', 'mem'), may hold values from -6 to 6
- well_cells: int32 [128], replicated, may hold values from 0 to 262143
- obs_data: float32 [128], replicated, may hold values from -6 to 6
- obs_var: float32 [128], replicated, may hold values from 0.05 to 0.5
- obs_noise: float32 [128, 128], P('mem'), may hold values from -6 to 6
Outputs:
- forecast: float32 [128, 128, 2048], P('space', 'mem')
- updated_log_perm: float32 [128, 128, 2048], P('space', 'mem')
Inputs may be any that keep to these rules, and one draw needn't show every extreme that they name: `well_cells`: cells flattened as row times 2048 plus column.
All inputs are finite; a program needn't handle non-finite values.
Results may differ from a plain program's by a relative error of at most 0.0034.
Values may be sent and summed in bfloat16 or wider, within the bound.
No kernel may reach another device: no remote copies, remote signals or barrier semaphores. Data moves between devices by JAX's collectives and lax.ppermute only.
A program may use at most 128 MiB of HBM per device.

v0:
```python
import jax
import jax.numpy as jnp
from jax import lax
from jax.sharding import PartitionSpec as P

time_step = 0.03
inflation = 4.0


def with_halo(block, sides, width):
    for axis, dim in sides:
        count = lax.axis_size(axis)
        forward = [(i, i + 1) for i in range(count - 1)]
        backward = [(target, source) for source, target in forward]
        low = lax.ppermute(
            lax.slice_in_dim(block, block.shape[dim] - width, None, axis=dim), axis, forward
        )
        high = lax.ppermute(lax.slice_in_dim(block, 0, width, axis=dim), axis, backward)
        block = jnp.concatenate([low, block, high], axis=dim)
    return block


def advance(conc_ext, conduct_ext):
    conc_pad = jnp.pad(conc_ext, ((0, 0), (0, 0), (1, 1)))
    cond_pad = jnp.pad(conduct_ext, ((0, 0), (0, 0), (1, 1)))
    centre = conc_pad[1:-1, :, 1:-1]
    centre_cond = cond_pad[1:-1, :, 1:-1]
    inflow = jnp.zeros_like(centre)
    sides = (
        (conc_pad[:-2, :, 1:-1], cond_pad[:-2, :, 1:-1]),
        (conc_pad[2:, :, 1:-1], cond_pad[2:, :, 1:-1]),
        (conc_pad[1:-1, :, :-2], cond_pad[1:-1, :, :-2]),
        (conc_pad[1:-1, :, 2:], cond_pad[1:-1, :, 2:]),
    )
    for conc_side, cond_side in sides:
        inflow = inflow + 0.5 * (centre_cond + cond_side) * (conc_side - centre)
    return centre + time_step * inflow


def cholesky_solve(matrix, target):
    factor = jnp.linalg.cholesky(matrix)
    middle = lax.linalg.triangular_solve(factor, target, left_side=True, lower=True)
    return lax.linalg.triangular_solve(factor, middle, left_side=True, lower=True, transpose_a=True)


def transform(predicted, noise_all, obs_data, obs_var):
    members = predicted.shape[0]
    anomaly = predicted - jnp.mean(predicted, axis=0, keepdims=True)
    covariance = jnp.dot(
        anomaly.T, anomaly, precision=lax.Precision.HIGHEST, preferred_element_type=jnp.float32
    ) / (members - 1) + inflation * jnp.diag(obs_var)
    innovation = obs_data[None, :] + jnp.sqrt(inflation * obs_var)[None, :] * noise_all - predicted
    solved = cholesky_solve(covariance, innovation.T)
    weights = jnp.dot(
        anomaly, solved, precision=lax.Precision.HIGHEST, preferred_element_type=jnp.float32
    ) / (members - 1)
    centred = weights - jnp.mean(weights, axis=0, keepdims=True)
    return centred.astype(jnp.bfloat16)


def local(log_perm, concentration, well_cells, obs_data, obs_var, obs_noise):
    row_count, member_dev, col_count = log_perm.shape
    tile_index = lax.axis_index("space")
    group_index = lax.axis_index("mem")
    conduct = jnp.exp(log_perm)
    tracer = concentration
    for repeat in range(2):
        padded = with_halo(jnp.stack([tracer, conduct]), (("space", 1),), 1)
        tracer = advance(padded[0], padded[1])
    first_cell = tile_index * (row_count * col_count)
    local_cell = well_cells - first_cell
    inside_tile = (local_cell >= 0) & (local_cell < row_count * col_count)
    clipped = jnp.clip(local_cell, 0, row_count * col_count - 1)
    picked = tracer[clipped // col_count, :, clipped % col_count]
    picked = jnp.where(inside_tile[:, None], picked, 0.0).T
    summed = lax.psum(picked, "space")
    predicted, noise_all = (
        lax.all_gather(summed, "mem", axis=0, tiled=True),
        lax.all_gather(obs_noise, "mem", axis=0, tiled=True),
    )
    centred = transform(predicted, noise_all, obs_data, obs_var)
    perm_low = log_perm.astype(jnp.bfloat16)
    my_columns = lax.dynamic_slice_in_dim(centred, group_index * member_dev, member_dev, 1)
    increment = jnp.einsum(
        "xiy,ij->xjy",
        lax.all_gather(perm_low, "mem", axis=1, tiled=True),
        my_columns,
        preferred_element_type=jnp.float32,
    )
    return (tracer, log_perm + increment)


def solution(mesh):
    return jax.shard_map(
        local,
        mesh=mesh,
        in_specs=(P("space", "mem", None), P("space", "mem", None), P(), P(), P(), P("mem", None)),
        out_specs=(P("space", "mem", None), P("space", "mem", None)),
        check_vma=False,
    )
```

profile of v0, /device:TPU:257, one launch (start us, length us, event | category | flops | bytes accessed | tf_op | source)
XLA Modules:
  0.0 546.4 jit_solution(17036058877172273697)
XLA Ops:
  7.2 0.0 all-gather.2.cloned.1.call-start
  7.2 1.0 exponential_bitcast_fusion
  8.2 1.0 fusion.10
  9.2 3.7 collective-permute-start.1
  12.9 1.9 collective-permute-start
  14.8 0.7 fusion.75
  15.5 0.0 copy-start
  15.5 2.8 collective-permute-done.1
  18.3 13.8 %collective-permute-done = f32[2,1,16,2048]{3,2,1,0:T(8,128)S(1)} collective-permute-done((f32[2,1,16,2048]{3,2,1,0:T(8,128)S(1)}, f32[2,1,16,2048]{3,2,1,0:T(8,128)S(1)}, u32[]{:S(2)}, u32[]{:S(2)}) %collective-permute-start) | collective-permute-done | bytes 262176 | tf_op jit(solution)/shard_map/ppermute | solution.py:15
  32.1 1.0 fusion.2
  33.1 0.0 copy-start.1
  33.2 0.1 slice_bitcast_fusion.2
  33.2 0.2 fusion.7
  33.4 0.0 copy-start.6
  33.4 0.0 copy-start.3
  33.5 0.0 copy-start.4
  33.5 0.6 copy-done.1
  34.1 0.9 fusion.79
  35.1 1.9 collective-permute-start.3
  37.0 3.4 collective-permute-start.2
  40.4 19.5 %all_gather.10 = f32[128,128]{1,0:T(8,128)S(1)} all-gather(f32[16,128]{1,0:T(8,128)S(1)} %copy-done.3), channel_id=1, replica_groups=mesh['mem'=8,'space'=64] {'mem'}, dimensions={0}, use_global_device_ids=true | all-gather | bytes 73728 | tf_op jit(solution)/shard_map/all_gather | solution.py:79
  59.9 0.0 all-gather.2.cloned.1.call-update
  59.9 0.0 collective-permute-done.3
  59.9 0.0 collective-permute-done.2
  60.0 0.1 fusion.4
  60.0 0.1 slice_bitcast_fusion
  60.1 0.2 fusion.8
  60.3 0.4 fusion.29
  60.7 0.0 copy-start.2
  60.7 0.0 copy-start.5
  60.7 0.6 copy.44
  61.3 1.2 gather_fusion
  62.5 0.1 select_bitcast_fusion
  62.6 381.0 %psum.7 = f32[16,128]{0,1:T(8,128)S(1)} all-reduce(f32[16,128]{0,1:T(8,128)S(1)} %select_bitcast_fusion), channel_id=1, replica_groups=mesh['mem'=8,'space'=64] {'space'}, use_global_device_ids=true, to_apply=%region_0.1 | all-reduce | flops 2048 | bytes 16384 | tf_op jit(solution)/shard_map/psum | solution.py:76
  443.6 0.1 copy.45
  443.7 69.2 %all_gather.9 = f32[128,128]{1,0:T(8,128)S(1)} all-gather(f32[16,128]{1,0:T(8,128)S(1)} %copy.45), channel_id=1, replica_groups=mesh['mem'=8,'space'=64] {'mem'}, dimensions={0}, use_global_device_ids=true | all-gather | bytes 73728 | tf_op jit(solution)/shard_map/all_gather | solution.py:78
  512.9 0.3 convolution_multiply_fusion.1
  513.2 0.1 copy.47
  513.3 0.1 fusion.59
  513.4 11.7 %cholesky.16 = f32[128,128]{1,0:T(8,128)S(1)} custom-call(f32[128,128]{1,0:T(8,128)S(1)} %fusion.59), custom_call_target="Cholesky" | custom-call | tf_op jit(solution)/shard_map/jit(cholesky)/cholesky | solution.py:41
  525.1 0.7 compare_reduce_fusion
  525.8 0.6 fusion.53
  526.5 9.8 %custom-call.8 = f32[1,128,128]{1,2,0:T(8,128)S(1)} custom-call(f32[1,128,128]{2,1,0:T(8,128)S(1)} %fusion.53), custom_call_target="InvertDiagBlocksLowerTriangular" | custom-call | tf_op jit(solution)/shard_map/triangular_solve | solution.py:43
  536.3 0.3 fusion.56
  536.6 0.2 fusion.54
  536.8 0.4 fusion.80
  537.2 0.1 dynamic-slice
  537.3 2.2 fusion
  (14 shorter events, 0.2 us)
Async XLA Ops:
  7.2 530.1 %all-gather.2.cloned.1.call-start = ((), (), s32[]{:S(2)}) async-start(), calls=%async_computation | async-start | bytes 1179648 | tf_op jit(solution)/shard_map/all_gather | solution.py:86
  9.2 9.1 %collective-permute-start.1 = (f32[2,1,16,2048]{3,2,1,0:T(8,128)S(1)}, f32[2,1,16,2048]{3,2,1,0:T(8,128)S(1)}, u32[]{:S(2)}, u32[]{:S(2)}) collective-permute-start(f32[2,1,16,2048]{3,2,1,0:T(8,128)S(1)} %get-tuple-element.17), channel_id=1, source_target_pairs={{1,0},{2,1},{3,2},{4,3},{5,4},{6,5},{7,6},{8,7},{9,8},{10,9},{11,1... | collective-permute-start | bytes 786440 | tf_op jit(solution)/shard_map/ppermute | solution.py:18
  12.9 19.2 %collective-permute-start = (f32[2,1,16,2048]{3,2,1,0:T(8,128)S(1)}, f32[2,1,16,2048]{3,2,1,0:T(8,128)S(1)}, u32[]{:S(2)}, u32[]{:S(2)}) collective-permute-start(f32[2,1,16,2048]{3,2,1,0:T(8,128)S(1)} %get-tuple-element.16), channel_id=1, source_target_pairs={{0,1},{1,2},{2,3},{3,4},{4,5},{5,6},{6,7},{7,8},{8,9},{9,10},{10,1... | collective-permute-start | bytes 786440 | tf_op jit(solution)/shard_map/ppermute | solution.py:15
  15.5 17.8 %copy-start = (f32[2,16,2048]{2,1,0:T(8,128)S(1)}, f32[2,16,2048]{2,1,0:T(8,128)}, u32[]{:S(2)}) copy-start(f32[2,16,2048]{2,1,0:T(8,128)} %param.7) | copy-start | bytes 786436
  33.1 1.0 copy-start.1
  33.4 7.0 %copy-start.6 = (s32[128]{0:T(128)S(1)}, s32[128]{0:T(128)}, u32[]{:S(2)}) copy-start(s32[128]{0:T(128)} %param.8) | copy-start | bytes 1540
  33.4 7.0 %copy-start.3 = (f32[16,128]{1,0:T(8,128)S(1)}, f32[16,128]{1,0:T(8,128)}, u32[]{:S(2)}) copy-start(f32[16,128]{1,0:T(8,128)} %param.11) | copy-start | bytes 24580
  33.5 26.4 %copy-start.4 = (f32[128]{0:T(128)S(1)}, f32[128]{0:T(128)}, u32[]{:S(2)}) copy-start(f32[128]{0:T(128)} %param.10) | copy-start | bytes 1540
  35.1 24.9 %collective-permute-start.3 = (f32[2,1,16,2048]{3,2,1,0:T(8,128)S(1)}, f32[2,1,16,2048]{3,2,1,0:T(8,128)S(1)}, u32[]{:S(2)}, u32[]{:S(2)}) collective-permute-start(f32[2,1,16,2048]{3,2,1,0:T(8,128)S(1)} %get-tuple-element.13), channel_id=1, source_target_pairs={{1,0},{2,1},{3,2},{4,3},{5,4},{6,5},{7,6},{8,7},{9,8},{10,9},{11,1... | collective-permute-start | bytes 786440 | tf_op jit(solution)/shard_map/ppermute | solution.py:18
  37.0 22.9 %collective-permute-start.2 = (f32[2,1,16,2048]{3,2,1,0:T(8,128)S(1)}, f32[2,1,16,2048]{3,2,1,0:T(8,128)S(1)}, u32[]{:S(2)}, u32[]{:S(2)}) collective-permute-start(f32[2,1,16,2048]{3,2,1,0:T(8,128)S(1)} %get-tuple-element.12), channel_id=1, source_target_pairs={{0,1},{1,2},{2,3},{3,4},{4,5},{5,6},{6,7},{7,8},{8,9},{9,10},{10,1... | collective-permute-start | bytes 786440 | tf_op jit(solution)/shard_map/ppermute | solution.py:15
  60.7 475.9 %copy-start.2 = (f32[2,16,2048]{2,1,0:T(8,128)}, f32[2,16,2048]{2,1,0:T(8,128)S(1)}, u32[]{:S(2)}) copy-start(f32[2,16,2048]{2,1,0:T(8,128)S(1)} %fusion.29) | copy-start | bytes 786436
  60.7 475.6 %copy-start.5 = (f32[128]{0:T(128)S(1)}, f32[128]{0:T(128)}, u32[]{:S(2)}) copy-start(f32[128]{0:T(128)} %param.9) | copy-start | bytes 1540
Sparse Core Ops, SparseCore 0:
  60.1 35.0 all-gather.1
where the time goes:
time: 547 us; the launch traced here: 546 us
  blocking collectives  470 us (86%)
  other arithmetic  27.6 us (5%)
  waiting for transfers between devices  16.6 us (3%)
  between operations  14.3 us (3%)
  starting transfers between devices  10.9 us (2%)
    psum x1, blocking collectives, local(): summed = lax.psum(picked, 'space')  381 us
    all_gather x1, blocking collectives, local(): lax.all_gather(summed, 'mem', axis=0, tiled=True)  69.2 us
    all_gather x1, blocking collectives, local(): lax.all_gather(obs_noise, 'mem', axis=0, tiled=True)  19.5 us
    ppermute x2, waiting for transfers between devices, with_halo(): lax.ppermute(lax.slice_in_dim(block, block.shape[dim] - width, None, axis...  13.8 us
    another operation x3, other arithmetic, cholesky_solve(): factor = jnp.linalg.cholesky(matrix)  12.4 us
  transfers between devices with their start and end apart: 5, of which 2 were waited for; matrix products, arithmetic and copies ran while one was open for 5% of the time, Pallas kernels for 0%

commit v1 on v0

--- a/solution.py
+++ b/solution.py
@@ -73,7 +73,7 @@
     clipped = jnp.clip(local_cell, 0, row_count * col_count - 1)
     picked = tracer[clipped // col_count, :, clipped % col_count]
     picked = jnp.where(inside_tile[:, None], picked, 0.0).T
-    summed = lax.psum(picked, "space")
+    summed = jnp.sum(lax.all_gather(picked, "space"), axis=0)
     predicted, noise_all = (
         lax.all_gather(summed, "mem", axis=0, tiled=True),
         lax.all_gather(obs_noise, "mem", axis=0, tiled=True),

time: 547 us -> 334 us (0.61)
  blocking collectives: 470 us -> 257 us
    psum x1 -> x0, blocking collectives: 381 us -> none  [local(): summed = lax.psum(picked, 'space')]
    all_gather x0 -> x1, blocking collectives: none -> 196 us  [local(): summed = jnp.sum(lax.all_gather(picked, 'space'), axis=0)]
    all_gather x1, blocking collectives: 69.2 us -> 41.5 us  [local(): lax.all_gather(summed, 'mem', axis=0, tiled=True)]
  transfers between devices with their start and end apart: 5 -> 5, of which waited for: 2 -> 2; matrix products, arithmetic and copies ran while one was open for 5% -> 8% of each run, Pallas kernels for 0% -> 0%
where the time goes in v1:
time: 334 us
  blocking collectives  257 us (77%)
  other arithmetic  27.7 us (8%)
  waiting for transfers between devices  16.6 us (5%)
  between operations  14.3 us (4%)
  starting transfers between devices  10.9 us (3%)
  local copies, waits for them, and re-layouts  3.87 us (1%)
  matrix products  3.39 us (1%)
    all_gather x1, blocking collectives, local(): summed = jnp.sum(lax.all_gather(picked, 'space'), axis=0)  196 us
    all_gather x1, blocking collectives, local(): lax.all_gather(summed, 'mem', axis=0, tiled=True)  41.5 us
    all_gather x1, blocking collectives, local(): lax.all_gather(obs_noise, 'mem', axis=0, tiled=True)  19.5 us
    ppermute x2, waiting for transfers between devices, with_halo(): lax.ppermute(lax.slice_in_dim(block, block.shape[dim] - width, None, axis...  13.8 us
    another operation x3, other arithmetic, cholesky_solve(): factor = jnp.linalg.cholesky(matrix)  12.4 us
    another operation x2, other arithmetic, cholesky_solve(): lax.linalg.triangular_solve(factor, middle, left_side=True, lower=True, t...  10.4 us
  transfers between devices with their start and end apart: 5, of which 2 were waited for; matrix products, arithmetic and copies ran while one was open for 8% of the time, Pallas kernels for 0%

profile of v1, /device:TPU:257, one launch (start us, length us, event | category | flops | bytes accessed | tf_op | source)
XLA Modules:
  0.0 333.8 jit_solution(12880356906473842103)
XLA Ops:
  7.2 0.0 all-gather.3.cloned.1.call-start
  7.2 1.0 exponential_bitcast_fusion
  8.2 1.0 fusion.10
  9.2 3.7 %collective-permute-start.1 = (f32[2,1,16,2048]{3,2,1,0:T(8,128)S(1)}, f32[2,1,16,2048]{3,2,1,0:T(8,128)S(1)}, u32[]{:S(2)}, u32[]{:S(2)}) collective-permute-start(f32[2,1,16,2048]{3,2,1,0:T(8,128)S(1)} %get-tuple-element.19), channel_id=1, source_target_pairs={{1,0},{2,1},{3,2},{4,3},{5,4},{6,5},{7,6},{8,7},{9,8},{10,9},{11,1... | collective-permute-start | bytes 786440 | tf_op jit(solution)/shard_map/ppermute | solution.py:18
  12.9 1.9 collective-permute-start
  14.8 0.7 fusion.75
  15.5 0.0 copy-start
  15.5 2.8 collective-permute-done.1
  18.3 13.8 %collective-permute-done = f32[2,1,16,2048]{3,2,1,0:T(8,128)S(1)} collective-permute-done((f32[2,1,16,2048]{3,2,1,0:T(8,128)S(1)}, f32[2,1,16,2048]{3,2,1,0:T(8,128)S(1)}, u32[]{:S(2)}, u32[]{:S(2)}) %collective-permute-start) | collective-permute-done | bytes 262176 | tf_op jit(solution)/shard_map/ppermute | solution.py:15
  32.1 1.0 fusion.2
  33.1 0.0 copy-start.1
  33.2 0.1 slice_bitcast_fusion.2
  33.2 0.2 fusion.7
  33.4 0.0 copy-start.6
  33.4 0.0 copy-start.3
  33.5 0.0 copy-start.4
  33.5 0.6 copy-done.1
  34.1 0.9 fusion.79
  35.1 1.9 collective-permute-start.3
  37.0 3.4 %collective-permute-start.2 = (f32[2,1,16,2048]{3,2,1,0:T(8,128)S(1)}, f32[2,1,16,2048]{3,2,1,0:T(8,128)S(1)}, u32[]{:S(2)}, u32[]{:S(2)}) collective-permute-start(f32[2,1,16,2048]{3,2,1,0:T(8,128)S(1)} %get-tuple-element.14), channel_id=1, source_target_pairs={{0,1},{1,2},{2,3},{3,4},{4,5},{5,6},{6,7},{7,8},{8,9},{9,10},{10,1... | collective-permute-start | bytes 786440 | tf_op jit(solution)/shard_map/ppermute | solution.py:15
  40.4 19.5 %all_gather.18 = f32[128,128]{1,0:T(8,128)S(1)} all-gather(f32[16,128]{1,0:T(8,128)S(1)} %copy-done.3), channel_id=1, replica_groups=mesh['mem'=8,'space'=64] {'mem'}, dimensions={0}, use_global_device_ids=true | all-gather | bytes 73728 | tf_op jit(solution)/shard_map/all_gather | solution.py:79
  59.9 0.0 all-gather.3.cloned.1.call-update
  59.9 0.0 collective-permute-done.2
  60.0 0.1 fusion.4
  60.0 0.1 slice_bitcast_fusion
  60.1 0.2 fusion.8
  60.3 0.4 fusion.29
  60.7 0.0 copy-start.2
  60.7 0.0 copy-start.5
  60.7 0.6 copy.54
  61.3 1.2 gather_fusion
  62.5 0.1 select_bitcast_fusion
  62.6 0.1 copy.55
  62.7 196.1 %all-gather = f32[1024,128]{1,0:T(8,128)S(1)} all-gather(f32[16,128]{1,0:T(8,128)S(1)} %copy.55), channel_id=2, replica_groups=mesh['mem'=8,'space'=64] {'space'}, dimensions={0}, use_global_device_ids=true | all-gather | bytes 532480 | tf_op jit(solution)/shard_map/all_gather | solution.py:76
  258.7 0.1 reduce_sum.27
  258.8 41.5 %all_gather.17 = f32[128,128]{1,0:T(8,128)S(1)} all-gather(f32[16,128]{1,0:T(8,128)S(1)} %reduce_sum.27), channel_id=1, replica_groups=mesh['mem'=8,'space'=64] {'mem'}, dimensions={0}, use_global_device_ids=true | all-gather | bytes 73728 | tf_op jit(solution)/shard_map/all_gather | solution.py:78
  300.3 0.3 convolution_multiply_fusion.1
  300.6 0.1 copy.57
  300.7 0.1 fusion.59
  300.8 11.7 %cholesky.16 = f32[128,128]{1,0:T(8,128)S(1)} custom-call(f32[128,128]{1,0:T(8,128)S(1)} %fusion.59), custom_call_target="Cholesky" | custom-call | tf_op jit(solution)/shard_map/jit(cholesky)/cholesky | solution.py:41
  312.6 0.7 compare_reduce_fusion
  313.3 0.6 fusion.53
  313.9 9.8 %custom-call.8 = f32[1,128,128]{1,2,0:T(8,128)S(1)} custom-call(f32[1,128,128]{2,1,0:T(8,128)S(1)} %fusion.53), custom_call_target="InvertDiagBlocksLowerTriangular" | custom-call | tf_op jit(solution)/shard_map/triangular_solve | solution.py:43
  323.7 0.3 fusion.56
  324.0 0.2 fusion.54
  324.2 0.4 fusion.80
  324.6 0.1 dynamic-slice
  324.7 2.2 fusion
  (15 shorter events, 0.2 us)
Async XLA Ops:
  7.2 317.5 %all-gather.3.cloned.1.call-start = ((), (), s32[]{:S(2)}) async-start(), calls=%async_computation | async-start | bytes 1179648 | tf_op jit(solution)/shard_map/all_gather | solution.py:86
  9.2 9.1 %collective-permute-start.1 = (f32[2,1,16,2048]{3,2,1,0:T(8,128)S(1)}, f32[2,1,16,2048]{3,2,1,0:T(8,128)S(1)}, u32[]{:S(2)}, u32[]{:S(2)}) collective-permute-start(f32[2,1,16,2048]{3,2,1,0:T(8,128)S(1)} %get-tuple-element.19), channel_id=1, source_target_pairs={{1,0},{2,1},{3,2},{4,3},{5,4},{6,5},{7,6},{8,7},{9,8},{10,9},{11,1... | collective-permute-start | bytes 786440 | tf_op jit(solution)/shard_map/ppermute | solution.py:18
  12.9 19.2 %collective-permute-start = (f32[2,1,16,2048]{3,2,1,0:T(8,128)S(1)}, f32[2,1,16,2048]{3,2,1,0:T(8,128)S(1)}, u32[]{:S(2)}, u32[]{:S(2)}) collective-permute-start(f32[2,1,16,2048]{3,2,1,0:T(8,128)S(1)} %get-tuple-element.18), channel_id=1, source_target_pairs={{0,1},{1,2},{2,3},{3,4},{4,5},{5,6},{6,7},{7,8},{8,9},{9,10},{10,1... | collective-permute-start | bytes 786440 | tf_op jit(solution)/shard_map/ppermute | solution.py:15
  15.5 17.8 %copy-start = (f32[2,16,2048]{2,1,0:T(8,128)S(1)}, f32[2,16,2048]{2,1,0:T(8,128)}, u32[]{:S(2)}) copy-start(f32[2,16,2048]{2,1,0:T(8,128)} %param.7) | copy-start | bytes 786436
  33.1 1.0 copy-start.1
  33.4 7.0 %copy-start.6 = (s32[128]{0:T(128)S(1)}, s32[128]{0:T(128)}, u32[]{:S(2)}) copy-start(s32[128]{0:T(128)} %param.8) | copy-start | bytes 1540
  33.4 7.0 %copy-start.3 = (f32[16,128]{1,0:T(8,128)S(1)}, f32[16,128]{1,0:T(8,128)}, u32[]{:S(2)}) copy-start(f32[16,128]{1,0:T(8,128)} %param.11) | copy-start | bytes 24580
  33.5 26.4 %copy-start.4 = (f32[128]{0:T(128)S(1)}, f32[128]{0:T(128)}, u32[]{:S(2)}) copy-start(f32[128]{0:T(128)} %param.10) | copy-start | bytes 1540
  35.1 24.9 %collective-permute-start.3 = (f32[2,1,16,2048]{3,2,1,0:T(8,128)S(1)}, f32[2,1,16,2048]{3,2,1,0:T(8,128)S(1)}, u32[]{:S(2)}, u32[]{:S(2)}) collective-permute-start(f32[2,1,16,2048]{3,2,1,0:T(8,128)S(1)} %get-tuple-element.15), channel_id=1, source_target_pairs={{1,0},{2,1},{3,2},{4,3},{5,4},{6,5},{7,6},{8,7},{9,8},{10,9},{11,1... | collective-permute-start | bytes 786440 | tf_op jit(solution)/shard_map/ppermute | solution.py:18
  37.0 22.9 %collective-permute-start.2 = (f32[2,1,16,2048]{3,2,1,0:T(8,128)S(1)}, f32[2,1,16,2048]{3,2,1,0:T(8,128)S(1)}, u32[]{:S(2)}, u32[]{:S(2)}) collective-permute-start(f32[2,1,16,2048]{3,2,1,0:T(8,128)S(1)} %get-tuple-element.14), channel_id=1, source_target_pairs={{0,1},{1,2},{2,3},{3,4},{4,5},{5,6},{6,7},{7,8},{8,9},{9,10},{10,1... | collective-permute-start | bytes 786440 | tf_op jit(solution)/shard_map/ppermute | solution.py:15
  60.7 198.1 %copy-start.2 = (f32[2,16,2048]{2,1,0:T(8,128)}, f32[2,16,2048]{2,1,0:T(8,128)S(1)}, u32[]{:S(2)}) copy-start(f32[2,16,2048]{2,1,0:T(8,128)S(1)} %fusion.29) | copy-start | bytes 786436
  60.7 263.0 %copy-start.5 = (f32[128]{0:T(128)S(1)}, f32[128]{0:T(128)}, u32[]{:S(2)}) copy-start(f32[128]{0:T(128)} %param.9) | copy-start | bytes 1540
Sparse Core Ops, SparseCore 0:
  60.1 35.0 all-gather.2
